TPU v7x, 32 devices: a whole 2x2x4 slice. The times are simulated.
32 devices in a mesh: space: 16 (over z, y, x), mem: 2 (over core).
Axes of the slice: x: 2, y: 2, z: 4, core: 2. Of those that a mesh axis runs over, the one named last changes fastest.
Arguments:
- perturb: float32 [1024, 4096], P(('space', 'mem')), may hold values from -6 to 6
- pair_list: int32 [64, 3], P('space'), may hold values from 0 to 15, as said below
- pair_count: int32 [16], P('space'), may hold values from 1 to 4, as said below
- band_weight: float32 [8], replicated, may hold values from 0.25 to 1
- cov_scale: float32 [1], replicated, may hold values from 0.5 to 2
- target: float32 [4096, 1024], P('space', 'mem'), may hold values from -6 to 6
- first_guess: float32 [4096, 1024], P('space', 'mem'), may hold values from -6 to 6
Outputs:
- solution: float32 [4096, 1024], P('space', 'mem')
Inputs may be any that keep to these rules, and one draw needn't show every extreme that they name: `pair_list`: rows 4 * s to 4 * s + 3 are owner s's slots. The first block of each is owner s's own block s; the second is the first plus d modulo 16, with 0 <= d <= 3; each of the four pairs (d = 0 to 3) stands in exactly one slot of its owner. The third column is an index into band_weight. Only the first pair_count[s] slots of owner s are live; in every draw some owner has all 4 slots live.
All inputs are finite; a program needn't handle non-finite values.
Results may differ from a plain program's by a relative error of at most 0.0003.
Values sent between devices are 32-bit elements; how exact they have to be, the bound alone decides.
A program may use at most 64 MiB of HBM per device.

v0:
```python
import functools
import jax
import jax.numpy as jnp
from jax import lax
from jax.experimental import pallas as pl
from jax.experimental.pallas import tpu as pltpu
from jax.sharding import PartitionSpec as P

BLOCK = 256
MEMBERS = 1024
REACH_DEV = 3
NBANDS = 8
ITERS = 2


def shifted(array, axis, by):
    count = lax.axis_size(axis)
    return lax.ppermute(array, axis, [(i, (i + by) % count) for i in range(count)])


def mm(a, b, ca, cb):
    return lax.dot_general(
        a, b, (((ca,), (cb,)), ((), ())), precision=lax.Precision.HIGH,
        preferred_element_type=jnp.float32,
    )


def member_sum(tile):
    if lax.axis_size("mem") == 2:
        return tile + shifted(tile, "mem", 1)
    return lax.psum(tile, "mem")


def gap_weights(pair_list, pair_count, band_weight, cov_scale):
    slots = pair_list.shape[0]
    blocks_all = lax.axis_size("space")
    gap = (pair_list[:, 1] - pair_list[:, 0]) % blocks_all
    living = (jnp.arange(slots, dtype=jnp.int32) < pair_count[0]).astype(jnp.float32)
    bands = jnp.arange(NBANDS, dtype=jnp.int32)
    band_now = jnp.sum(
        jnp.where(pair_list[:, 2][:, None] == bands[None, :], band_weight[None, :], 0.0), axis=1
    )
    slot_weight = cov_scale[0] * band_now * living / (MEMBERS - 1)
    gaps = jnp.arange(REACH_DEV + 1, dtype=jnp.int32)
    return jnp.sum(jnp.where(gap[:, None] == gaps[None, :], slot_weight[:, None], 0.0), axis=0)


def by_collectives(perturb, pair_list, pair_count, band_weight, cov_scale, target, first_guess):
    w = gap_weights(pair_list, pair_count, band_weight, cov_scale)
    w_next = shifted(w, "space", -1)
    p0 = lax.all_to_all(perturb, "space", split_axis=1, concat_axis=0, tiled=True)
    p1 = shifted(p0, "space", -1)
    p3 = shifted(p0, "space", -3)
    x0 = first_guess
    t0 = mm(p0, p0, 0, 0) * w[0]
    t1 = mm(p0, p1, 0, 0) * w[1]
    t3 = mm(p0, p3, 0, 0) * w[3]
    t2 = mm(p1, p3, 0, 0) * w_next[2]
    t0, t1, t2, t3 = (member_sum(t) for t in (t0, t1, t2, t3))
    for sweep in range(ITERS):
        x1 = shifted(x0, "space", -1)
        x3 = shifted(x0, "space", -3)
        back1 = shifted(mm(t1, x0, 0, 0) + mm(t2, x3, 1, 0), "space", 1)
        back3 = shifted(mm(t3, x0, 0, 0) + mm(t2, x1, 0, 0), "space", 3)
        own = mm(t0, x0, 1, 0) + mm(t1, x1, 1, 0) + mm(t3, x3, 1, 0)
        x0 = x0 + 0.5 * (target - x0 - (own + back1 + back3))
    return x0

GROUP = REACH_DEV + 1
NEAR = 2 * REACH_DEV + 1
SPANS = ((0, 0), (1, 1), (3, 2))


class Mover:
    def __init__(self, send_sem, recv_sem, local_sem):
        self.send_sem, self.recv_sem, self.local_sem = send_sem, recv_sem, local_sem
        self.sent = 0
        self.local = 0
        self.open = []

    def to(self, source, target, device):
        copy = pltpu.make_async_remote_copy(
            src_ref=source, dst_ref=target,
            send_sem=self.send_sem.at[self.sent], recv_sem=self.recv_sem.at[self.sent],
            device_id=device, device_id_type=pl.DeviceIdType.MESH,
        )
        self.sent += 1
        copy.start()
        self.open.append(copy)
        return copy

    def here(self, source, target):
        copy = pltpu.make_async_copy(source, target, self.local_sem.at[self.local])
        self.local += 1
        copy.start()
        return copy


def split(value):
    high = value.astype(jnp.bfloat16)
    return high, (value - high.astype(jnp.float32)).astype(jnp.bfloat16)


def dot(a, b, ca, cb):
    return lax.dot_general(a, b, (((ca,), (cb,)), ((), ())), preferred_element_type=jnp.float32)


def kernel(planes, perturb, table, guess, target, out, pz, pg, part, part_in, table_next, tiles,
           tile_hi, tile_lo, xb, tb, halo, xs, acc, px, ret_in, halo_in, final, send_sem, recv_sem,
           local_sem):
    space = lax.axis_index("space")
    mem = lax.axis_index("mem")
    count = planes * GROUP
    k = space // GROUP
    j = space % GROUP
    rows = perturb.shape[0]
    width = GROUP * BLOCK
    cols = xb.shape[2]
    half = BLOCK // 2

    def plane(r):
        return (((k + r) % planes) * GROUP + j, mem)

    def chip(q):
        return (k * GROUP + (j + q) % GROUP, mem)

    partner = (space, 1 - mem)
    before = ((space + count - 1) % count, mem)
    after = ((space + 1) % count, mem)
    barrier = pltpu.get_barrier_semaphore()
    greeted = [plane(r) for r in range(1, planes)] + [chip(q) for q in range(1, GROUP)]
    greeted += [partner, before, after]
    for device in greeted:
        pl.semaphore_signal(barrier, inc=1, device_id=device, device_id_type=pl.DeviceIdType.MESH)
    pl.semaphore_wait(barrier, len(greeted))

    move = Mover(send_sem, recv_sem, local_sem)

    def at(block, size):
        return pl.ds(pl.multiple_of(block * BLOCK, BLOCK), size * BLOCK)

    from_plane = {}
    for r in range(planes - 1, 0, -1):
        there = (k + planes - r) % planes
        nxt = (there + 1) % planes
        device = plane(planes - r)
        from_plane[r] = (
            move.to(perturb.at[:, at(there * GROUP, GROUP)], pz.at[r, :, pl.ds(0, width)], device),
            move.to(perturb.at[:, at(nxt * GROUP, REACH_DEV)],
                    pz.at[r, :, pl.ds(width, REACH_DEV * BLOCK)], device),
        )
    table_copy = move.to(table, table_next, before)
    own = (
        move.here(perturb.at[:, at(k * GROUP, GROUP)], pz.at[0, :, pl.ds(0, width)]),
        move.here(perturb.at[:, at(((k + 1) % planes) * GROUP, REACH_DEV)],
                  pz.at[0, :, pl.ds(width, REACH_DEV * BLOCK)]),
    )
    for copy in own:
        copy.wait()

    def spread(r):
        copies = []
        for q in range(1, GROUP):
            there = (j + q) % GROUP
            copies.append(move.to(pz.at[r, :, at(there, 2)],
                                  pg.at[r, q, :, pl.ds(0, 2 * BLOCK)], chip(q)))
            copies.append(move.to(pz.at[r, :, at(there + REACH_DEV, 1)],
                                  pg.at[r, q, :, pl.ds(2 * BLOCK, BLOCK)], chip(q)))
        mine = (move.here(pz.at[r, :, at(j, 2)], pg.at[r, 0, :, pl.ds(0, 2 * BLOCK)]),
                move.here(pz.at[r, :, at(j + REACH_DEV, 1)],
                          pg.at[r, 0, :, pl.ds(2 * BLOCK, BLOCK)]))
        return copies, mine

    def products(r, copies):
        for copy in copies[0]:
            copy.wait_recv()
        for copy in copies[1]:
            copy.wait()
        value = pg[r].reshape(GROUP * rows, 3 * BLOCK)
        high, low = split(value)
        left = jnp.concatenate([high[:, : 2 * BLOCK], high[:, : 2 * BLOCK], low[:, : 2 * BLOCK]], 0)
        right = jnp.concatenate([high, low, high], 0)
        wide = dot(left[:, :BLOCK], right, 0, 0)
        last = dot(left[:, BLOCK:], right[:, 2 * BLOCK :], 0, 0)
        if r == 0:
            part[:, : 3 * BLOCK] = wide
            part[:, 3 * BLOCK :] = last
        else:
            part[:, : 3 * BLOCK] += wide
            part[:, 3 * BLOCK :] += last

    spreading = {0: spread(0)}

    def share(source, blocks):
        copies = []
        for q in range(1, GROUP):
            there = (j + q) % GROUP
            piece = source.at[:, pl.ds(pl.multiple_of(there * cols, cols), cols)]
            copies.append(move.to(piece, blocks.at[j], chip(q)))
        mine = move.here(source.at[:, pl.ds(pl.multiple_of(j * cols, cols), cols)], blocks.at[j])
        return copies, mine

    guesses = share(guess, xb)
    targets = share(target, tb)
    order = list(range(1, planes))
    for r in order:
        for copy in from_plane[r]:
            copy.wait_recv()
        spreading[r] = spread(r)
        products(r - 1, spreading[r - 1])
    for copy in guesses[0]:
        copy.wait_recv()
    guesses[1].wait()
    halo_copy = move.to(xb.at[pl.ds(0, REACH_DEV)], halo, plane(planes - 1))
    for n in range(GROUP):
        xs[n, :, :cols], xs[n, :, cols:] = split(xb[n])
    products(planes - 1, spreading[planes - 1])

    mine = pl.ds(pl.multiple_of(mem * half, half), half)
    other = pl.ds(pl.multiple_of((1 - mem) * half, half), half)
    part_copy = move.to(part.at[other], part_in, partner)
    table_copy.wait_recv()
    part_copy.wait_recv()
    rates = (table[0:1], table[1:2], table[3:4], table_next[2:3])
    for n, rate in enumerate(rates):
        span = pl.ds(n * BLOCK, BLOCK)
        tiles[j, mine, span] = (part[mine, span] + part_in[:, span]) * rate
    side = j + 1 - 2 * (j % 2)
    over = (j + 2) % GROUP
    far = (side + 2) % GROUP

    def tile_to(i, device):
        return move.to(tiles.at[i, mine], tiles.at[i, mine], device)

    near_copies = [tile_to(j, (k * GROUP + there, mem)) for there in (side, over)]
    pair = {0: tile_to(j, partner)}

    halo_copy.wait_recv()
    for n in range(REACH_DEV):
        xs[GROUP + n, :, :cols], xs[GROUP + n, :, cols:] = split(halo[n])
    for n in range(NEAR):
        acc[0, n] = jnp.zeros_like(acc[0, n])
        acc[1, n] = jnp.zeros_like(acc[1, n])

    def times(high, low, x, side):
        both = dot(high, x, side, 0)
        return both[:, :cols] + both[:, cols:] + dot(low, x[:, :cols], side, 0)

    def apply(sweep, i):
        xa, xb_, xc = xs[i], xs[i + 1], xs[i + 3]
        high, low = tile_hi[i], tile_lo[i]
        B = BLOCK
        acc[sweep, i] += (times(high[:, :B], low[:, :B], xa, 1)
                          + times(high[:, B : 2 * B], low[:, B : 2 * B], xb_, 1)
                          + times(high[:, 2 * B : 3 * B], low[:, 2 * B : 3 * B], xc, 1))
        down = times(high[:, B : 3 * B], low[:, B : 3 * B], xa, 0)
        acc[sweep, i + 1] += down[:B] + times(high[:, 3 * B :], low[:, 3 * B :], xc, 1)
        acc[sweep, i + 3] += down[B:] + times(high[:, 3 * B :], low[:, 3 * B :], xb_, 0)

    def take(step, i):
        pair[step].wait_recv()
        tile_hi[i], tile_lo[i] = split(tiles[i])
        apply(0, i)

    take(0, j)
    for copy in near_copies:
        copy.wait_recv()
    onward = tile_to(side + mem * (over - side), (k * GROUP + over + mem * (side - over), mem))
    pair[1] = tile_to(side, partner)
    pair[2] = tile_to(over, partner)
    take(1, side)
    take(2, over)
    onward.wait_recv()
    pair[3] = tile_to(far, partner)
    take(3, far)

    for copy in targets[0]:
        copy.wait_recv()
    targets[1].wait()
    def back(sweep, n):
        return move.to(acc.at[sweep, GROUP + n], ret_in.at[sweep, n], plane(1))

    backs = [back(0, n) for n in range(2)]
    aheads = []
    for n in range(GROUP):
        px[n] = xb[n] + 0.5 * (tb[n] - xb[n] - acc[0, n])
        if n < REACH_DEV:
            aheads.append(move.to(px.at[n], halo_in.at[n], plane(planes - 1)))
    backs.append(back(0, 2))

    def settle(n, now):
        xs[n, :, :cols], xs[n, :, cols:] = split(now)
        if n < GROUP:
            final[n] = now + 0.5 * (tb[n] - now)

    def settle_own(n):
        backs[n].wait_recv()
        settle(n, px[n] - 0.5 * ret_in[0, n])

    def settle_halo(n):
        aheads[n].wait_recv()
        settle(GROUP + n, halo_in[n] - 0.5 * acc[0, GROUP + n])

    place = pl.ds(pl.multiple_of(j * cols, cols), cols)
    base = move.sent
    here_sem = local_sem.at[move.local]

    def leave(n, source):
        return pltpu.make_async_remote_copy(
            src_ref=final.at[n], dst_ref=out.at[:, place],
            send_sem=send_sem.at[base + n], recv_sem=recv_sem.at[base + source],
            device_id=(k * GROUP + n, mem), device_id_type=pl.DeviceIdType.MESH,
        )

    def stay(n):
        return pltpu.make_async_copy(final.at[n], out.at[:, place], here_sem)

    def put(n):
        @pl.when(j != n)
        def _():
            leave(n, j).start()

        @pl.when(j == n)
        def _():
            stay(n).start()

    move.sent = base + GROUP
    settle(GROUP - 1, px[GROUP - 1])
    settle_own(0)
    settle_own(1)
    apply(1, 0)
    settle_own(2)
    settle_halo(0)
    apply(1, 1)
    settle_halo(1)
    apply(1, 2)
    backs = {1: back(1, 1)}
    settle_halo(2)
    apply(1, 3)
    backs[0] = back(1, 0)
    backs[2] = back(1, 2)
    final[3] = final[3] - 0.5 * acc[1, 3]
    put(3)
    for n in (1, 0, 2):
        backs[n].wait_recv()
        final[n] = final[n] - 0.5 * (acc[1, n] + ret_in[1, n])
        put(n)
    for n in range(GROUP):
        @pl.when(j != n)
        def _():
            leave(n, n).wait_send()
            leave(n, n).wait_recv()

        @pl.when(j == n)
        def _():
            stay(n).wait()
    for copy in move.open:
        copy.wait_send()


def in_one_kernel(perturb, pair_list, pair_count, band_weight, cov_scale, target, first_guess):
    w = gap_weights(pair_list, pair_count, band_weight, cov_scale)
    table = jnp.broadcast_to(jnp.pad(w, (0, 8 - w.shape[0]))[:, None], (8, BLOCK))
    planes = lax.axis_size("space") // GROUP
    rows = perturb.shape[0]
    cols = first_guess.shape[1] // GROUP
    f32, bf16 = jnp.float32, jnp.bfloat16
    sends = 2 * (planes - 1) + 1 + planes * 2 * (GROUP - 1) + 2 * (GROUP - 1) + 1 + 1
    sends += 3 + GROUP + 1 + 3 * REACH_DEV + GROUP
    locals_ = 2 + 2 * planes + 2 + 1
    vmem = pl.BlockSpec(memory_space=pltpu.VMEM)
    return pl.pallas_call(
        functools.partial(kernel, planes),
        out_shape=jax.ShapeDtypeStruct(first_guess.shape, f32),
        in_specs=[vmem] * 4,
        out_specs=vmem,
        scratch_shapes=[
            pltpu.VMEM((planes, rows, NEAR * BLOCK), f32),
            pltpu.VMEM((planes, GROUP, rows, 3 * BLOCK), f32),
            pltpu.VMEM((BLOCK, 4 * BLOCK), f32),
            pltpu.VMEM((BLOCK // 2, 4 * BLOCK), f32),
            pltpu.VMEM((8, BLOCK), f32),
            pltpu.VMEM((GROUP, BLOCK, 4 * BLOCK), f32),
            pltpu.VMEM((GROUP, BLOCK, 4 * BLOCK), bf16),
            pltpu.VMEM((GROUP, BLOCK, 4 * BLOCK), bf16),
            pltpu.VMEM((GROUP, BLOCK, cols), f32),
            pltpu.VMEM((GROUP, BLOCK, cols), f32),
            pltpu.VMEM((REACH_DEV, BLOCK, cols), f32),
            pltpu.VMEM((NEAR, BLOCK, 2 * cols), bf16),
            pltpu.VMEM((2, NEAR, BLOCK, cols), f32),
            pltpu.VMEM((GROUP, BLOCK, cols), f32),
            pltpu.VMEM((2, REACH_DEV, BLOCK, cols), f32),
            pltpu.VMEM((REACH_DEV, BLOCK, cols), f32),
            pltpu.VMEM((GROUP, BLOCK, cols), f32),
            pltpu.SemaphoreType.DMA((sends,)),
            pltpu.SemaphoreType.DMA((sends,)),
            pltpu.SemaphoreType.DMA((locals_,)),
        ],
        compiler_params=pltpu.CompilerParams(
            collective_id=0, has_side_effects=True, vmem_limit_bytes=48 * 1024 * 1024
        ),
    )(perturb, table, first_guess, target)


def fits(perturb, field):
    planes, rest = divmod(lax.axis_size("space"), GROUP)
    return (
        lax.axis_size("mem") == 2 and rest == 0 and planes >= 2
        and perturb.shape[0] % 8 == 0 and field.shape[1] % (GROUP * 128) == 0
        and field.shape[0] == BLOCK
    )


def per_device(perturb, pair_list, pair_count, band_weight, cov_scale, target, first_guess):
    whole = in_one_kernel if fits(perturb, first_guess) else by_collectives
    return whole(perturb, pair_list, pair_count, band_weight, cov_scale, target, first_guess)


def solution(mesh):
    in_specs = (
        P(("space", "mem"), None),
        P("space", None),
        P("space"),
        P(),
        P(),
        P("space", "mem"),
        P("space", "mem"),
    )
    out_specs = P("space", "mem")
    return jax.shard_map(
        per_device, mesh=mesh, in_specs=in_specs, out_specs=out_specs, check_vma=False
    )
```

profile of v0, /device:TPU:8, one launch (start us, length us, event | category | flops | bytes accessed | tf_op | source)
XLA Modules:
  0.0 103.5 jit_solution(12509003940542910515)
XLA Ops:
  0.7 0.0 copy-start.3
  1.3 0.0 copy-done.3
  1.3 0.2 fusion.1
  1.6 0.0 copy-start.4
  1.6 0.7 copy-done.4
  2.2 0.2 select_reduce_fusion.1
  2.4 0.1 select_reduce_fusion
  2.5 0.1 broadcast_in_dim.39.table
  2.6 0.0 copy-start
  2.6 1.0 %copy-done = f32[32,4096]{1,0:T(8,128)S(1)} copy-done((f32[32,4096]{1,0:T(8,128)S(1)}, f32[32,4096]{1,0:T(8,128)}, u32[]{:S(2)}) %copy-start) | copy-done | bytes 524312
  3.6 0.0 copy-start.1
  3.6 1.0 %copy-done.1 = f32[256,512]{1,0:T(8,128)S(1)} copy-done((f32[256,512]{1,0:T(8,128)S(1)}, f32[256,512]{1,0:T(8,128)}, u32[]{:S(2)}) %copy-start.1) | copy-done | bytes 524312
  4.7 0.0 copy-start.2
  4.7 1.0 %copy-done.2 = f32[256,512]{1,0:T(8,128)S(1)} copy-done((f32[256,512]{1,0:T(8,128)S(1)}, f32[256,512]{1,0:T(8,128)}, u32[]{:S(2)}) %copy-start.2) | copy-done | bytes 524312
  5.7 97.0 %shard_map.73 = f32[256,512]{1,0:T(8,128)S(1)} custom-call(f32[32,4096]{1,0:T(8,128)S(1)} %copy-done, f32[8,256]{1,0:T(8,128)S(1)} %broadcast_in_dim.39.table, f32[256,512]{1,0:T(8,128)S(1)} %copy-done.1, f32[256,512]{1,0:T(8,128)S(1)} %copy-done.2), custom_call_target="tpu_custom_call" | custom-call | tf_op jit(solution)/shard_map/pallas_call | solution.py:372
  102.7 0.8 copy.11
  (2 shorter events, 0.0 us)
Async XLA Ops:
  0.7 0.7 copy-start.3
  1.6 0.7 copy-start.4
  2.6 1.0 %copy-start = (f32[32,4096]{1,0:T(8,128)S(1)}, f32[32,4096]{1,0:T(8,128)}, u32[]{:S(2)}) copy-start(f32[32,4096]{1,0:T(8,128)} %perturb.1) | copy-start | bytes 1572868
  3.6 1.0 %copy-start.1 = (f32[256,512]{1,0:T(8,128)S(1)}, f32[256,512]{1,0:T(8,128)}, u32[]{:S(2)}) copy-start(f32[256,512]{1,0:T(8,128)} %guess.1) | copy-start | bytes 1572868
  4.7 1.0 %copy-start.2 = (f32[256,512]{1,0:T(8,128)S(1)}, f32[256,512]{1,0:T(8,128)}, u32[]{:S(2)}) copy-start(f32[256,512]{1,0:T(8,128)} %target.1) | copy-start | bytes 1572868
where the time goes:
time: 105 us; the launch traced here: 104 us
  Pallas kernels  97 us (92%)
  local copies, waits for them, and re-layouts  4.67 us (4%)
  between operations  1.34 us (1%)
    pallas_call x1, Pallas kernels, in_one_kernel(): pl.pallas_call(functools.partial(kernel, planes), out_shape=jax.ShapeDtyp...  97 us
    unnamed x11, local copies, waits for them, and re-layouts  4.59 us

commit v1 on v0

v1 whole, which is shorter than its diff:
```python
import functools
import jax
import jax.numpy as jnp
from jax import lax
from jax.experimental import pallas as pl
from jax.experimental.pallas import tpu as pltpu
from jax.sharding import PartitionSpec as P

BLOCK = 256
MEMBERS = 1024
REACH_DEV = 3
NBANDS = 8
ITERS = 2


def shifted(array, axis, by):
    count = lax.axis_size(axis)
    return lax.ppermute(array, axis, [(i, (i + by) % count) for i in range(count)])


def mm(a, b, ca, cb):
    return lax.dot_general(
        a, b, (((ca,), (cb,)), ((), ())), precision=lax.Precision.HIGH,
        preferred_element_type=jnp.float32,
    )


def member_sum(tile):
    if lax.axis_size("mem") == 2:
        return tile + shifted(tile, "mem", 1)
    return lax.psum(tile, "mem")


def gap_weights(pair_list, pair_count, band_weight, cov_scale):
    slots = pair_list.shape[0]
    blocks_all = lax.axis_size("space")
    gap = (pair_list[:, 1] - pair_list[:, 0]) % blocks_all
    living = (jnp.arange(slots, dtype=jnp.int32) < pair_count[0]).astype(jnp.float32)
    bands = jnp.arange(NBANDS, dtype=jnp.int32)
    band_now = jnp.sum(
        jnp.where(pair_list[:, 2][:, None] == bands[None, :], band_weight[None, :], 0.0), axis=1
    )
    slot_weight = cov_scale[0] * band_now * living / (MEMBERS - 1)
    gaps = jnp.arange(REACH_DEV + 1, dtype=jnp.int32)
    return jnp.sum(jnp.where(gap[:, None] == gaps[None, :], slot_weight[:, None], 0.0), axis=0)


def by_collectives(perturb, pair_list, pair_count, band_weight, cov_scale, target, first_guess):
    w = gap_weights(pair_list, pair_count, band_weight, cov_scale)
    w_next = shifted(w, "space", -1)
    p0 = lax.all_to_all(perturb, "space", split_axis=1, concat_axis=0, tiled=True)
    p1 = shifted(p0, "space", -1)
    p3 = shifted(p0, "space", -3)
    x0 = first_guess
    t0 = mm(p0, p0, 0, 0) * w[0]
    t1 = mm(p0, p1, 0, 0) * w[1]
    t3 = mm(p0, p3, 0, 0) * w[3]
    t2 = mm(p1, p3, 0, 0) * w_next[2]
    t0, t1, t2, t3 = (member_sum(t) for t in (t0, t1, t2, t3))
    for sweep in range(ITERS):
        x1 = shifted(x0, "space", -1)
        x3 = shifted(x0, "space", -3)
        back1 = shifted(mm(t1, x0, 0, 0) + mm(t2, x3, 1, 0), "space", 1)
        back3 = shifted(mm(t3, x0, 0, 0) + mm(t2, x1, 0, 0), "space", 3)
        own = mm(t0, x0, 1, 0) + mm(t1, x1, 1, 0) + mm(t3, x3, 1, 0)
        x0 = x0 + 0.5 * (target - x0 - (own + back1 + back3))
    return x0

GROUP = REACH_DEV + 1
NEAR = 2 * REACH_DEV + 1
PLANES = 4


def split(value):
    high = value.astype(jnp.bfloat16)
    return high, (value - high.astype(jnp.float32)).astype(jnp.bfloat16)


def dot(a, b, ca, cb):
    return lax.dot_general(a, b, (((ca,), (cb,)), ((), ())), preferred_element_type=jnp.float32)


class Mover:
    def __init__(self, send_sem, recv_sem, local_sem):
        self.send_sem, self.recv_sem, self.local_sem = send_sem, recv_sem, local_sem
        self.used = 0
        self.local = 0
        self.open = []

    def reserve(self, number):
        first = self.used
        self.used += number
        return first

    def make(self, source, target, device, send, recv):
        return pltpu.make_async_remote_copy(
            src_ref=source, dst_ref=target,
            send_sem=self.send_sem.at[send], recv_sem=self.recv_sem.at[recv],
            device_id=device, device_id_type=pl.DeviceIdType.MESH,
        )

    def to(self, source, target, device, send=None, recv=None):
        if send is None:
            send = recv = self.reserve(1)
        copy = self.make(source, target, device, send, recv)
        copy.start()
        self.open.append(copy)
        return copy

    def here(self, source, target):
        copy = pltpu.make_async_copy(source, target, self.local_sem.at[self.local])
        self.local += 1
        copy.start()
        return copy


def kernel(perturb, table, guess, target, out, gc, gb, chi, clo, bhi, blo, part, tile_hi, tile_lo,
           tabs, xb, tb, halo, xs, acc, px, ret_in, ahead, final, send_sem, recv_sem, local_sem):
    space = lax.axis_index("space")
    mem = lax.axis_index("mem")
    k = space // GROUP
    j = space % GROUP
    rows = perturb.shape[0]
    half = rows // 2
    cols = xb.shape[2]
    B = BLOCK
    wide = REACH_DEV * B
    inner = GROUP * B
    each = 2 * GROUP * rows

    def plane(p):
        return (p * GROUP + j, mem)

    def chip(q):
        return (k * GROUP + q, mem)

    xn = chip(j + 1 - 2 * (j % 2))
    yn = chip((j + 2) % GROUP)
    partner = (space, 1 - mem)
    before = plane((k + PLANES - 1) % PLANES)
    after = plane((k + 1) % PLANES)

    barrier = pltpu.get_barrier_semaphore()
    greeted = [plane((k + r) % PLANES) for r in range(1, PLANES)]
    greeted += [chip((j + q) % GROUP) for q in range(1, GROUP)] + [partner]
    for device in greeted:
        pl.semaphore_signal(barrier, inc=1, device_id=device, device_id_type=pl.DeviceIdType.MESH)

    move = Mover(send_sem, recv_sem, local_sem)

    def at(block, size):
        return pl.ds(pl.multiple_of(block * B, B), size * B)

    def piece(q):
        return pl.ds(pl.multiple_of(q * cols, cols), cols)

    def pieces(p, slot):
        first = p * GROUP
        after_first = ((p + 1) % PLANES) * GROUP
        return (
            (perturb.at[:, at(first + 1, REACH_DEV)], gc.at[slot, 0, 0, :, pl.ds(0, wide)]),
            (perturb.at[:, at(after_first, REACH_DEV)], gc.at[slot, 0, 0, :, pl.ds(wide, wide)]),
            (perturb.at[:, at(first, 1)], gb.at[0, 0, slot]),
        )

    own_here = [move.here(*pair) for pair in pieces(k, 0)]
    x_here = move.here(guess.at[:, piece(j)], xb.at[j])
    t_here = move.here(target.at[:, piece(j)], tb.at[j])
    tab_here = move.here(table, tabs.at[j])
    pl.semaphore_wait(barrier, len(greeted))

    zsem = move.reserve(3 * PLANES)
    other_half = 2 - 2 * (k // 2)
    late = 2 + (k + k // 2 + 1) % 2
    routes = ((k + 1 - 2 * (k % 2), 1), (other_half, late), (other_half + 1, late))

    def exchange(which):
        for n, (p, slot) in enumerate(routes):
            for m in which:
                source, place = pieces(p, slot)[m]
                move.to(source, place, plane(p), zsem + 3 * n + m, zsem + 3 * slot + m)

    def from_plane(slot, which):
        for m in which:
            place = pieces(k, slot)[m][1]
            move.make(place, place, before, zsem, zsem + 3 * slot + m).wait_recv()

    exchange((0, 1))
    for copy in own_here:
        copy.wait()

    class Gather:
        def __init__(self, buffer, cut):
            self.buffer, self.cut = buffer, cut

        def own(self):
            source = self.buffer.at[0, 0]
            self.cx = move.to(source, self.buffer.at[1, 0], xn)
            self.cy = move.to(source, self.buffer.at[2, 0], yn)
            self.done = [move.to(source, self.buffer.at[0, 1], partner)]

        def over(self, q):
            self.done.append(move.to(self.buffer.at[q, 0], self.buffer.at[q, 1], partner))

        def relay(self):
            low, high = pl.ds(0, self.cut), pl.ds(self.cut, self.cut)
            self.cx.wait_recv()
            first = move.to(self.buffer.at[1, 0, low], self.buffer.at[3, 0, low], yn)
            self.over(1)
            self.cy.wait_recv()
            second = move.to(self.buffer.at[2, 0, high], self.buffer.at[3, 0, high], xn)
            self.over(2)
            self.halves = (first, second)

        def corner(self):
            for copy in self.halves:
                copy.wait_recv()
            self.over(3)

        def ready(self):
            for copy in self.done:
                copy.wait_recv()

    cross = [Gather(gc.at[r], half) for r in range(PLANES)]
    edge = Gather(gb, PLANES // 2)
    cross[0].own()
    tab_here.wait()
    tab_copies = [move.to(tabs.at[j], tabs.at[j], chip((j + q) % GROUP)) for q in range(1, GROUP)]

    def share(source, blocks):
        copies = []
        for q in range(1, GROUP):
            there = (j + q) % GROUP
            copies.append(move.to(source.at[:, piece(there)], blocks.at[j], chip(there)))
        return copies

    x_copies = share(guess, xb)
    exchange((2,))

    def weight(a, d):
        return tabs[a, d : d + 1]

    def products(r):
        span = pl.ds(r * each, each)
        chi[span], clo[span] = split(gc[r].reshape(each, 2 * wide))

        def step(n, carry):
            own = pl.ds(pl.multiple_of(n * B, B), B)
            row = pl.ds(pl.multiple_of(n * B, B), inner)
            left = jnp.concatenate([chi[span, own], chi[span, own], clo[span, own]], 0)
            right = jnp.concatenate([chi[span, row], clo[span, row], chi[span, row]], 0)
            value = dot(left, right, 0, 0)
            if r > 0:
                value = value + part[n]
            if r < PLANES - 1:
                part[n] = value
            else:
                for d in range(GROUP):
                    now = value[:, d * B : (d + 1) * B] * weight(n + 1, d)
                    there = pl.ds(d * B, B)
                    tile_hi[n + 1, :, there], tile_lo[n + 1, :, there] = split(now)
            return carry

        lax.fori_loop(0, REACH_DEV, step, 0)

    def edge_products():
        for r in range(PLANES):
            span = pl.ds(r * each, each)
            bhi[span], blo[span] = split(gb[:, :, r].reshape(each, B))
        left = jnp.concatenate([bhi[...], bhi[...], blo[...]], 0)
        right = jnp.concatenate([bhi[...], blo[...], bhi[...]], 0)
        now = dot(left, right, 0, 0) * weight(0, 0)
        tile_hi[0, :, :B], tile_lo[0, :, :B] = split(now)
        for d in range(1, GROUP):
            there = pl.ds((d - 1) * B, B)
            right = jnp.concatenate([chi[:, there], clo[:, there], chi[:, there]], 0)
            now = dot(left, right, 0, 0) * weight(0, d)
            place = pl.ds(d * B, B)
            tile_hi[0, :, place], tile_lo[0, :, place] = split(now)

    def times(high, low, x, side):
        both = dot(high, x, side, 0)
        return both[:, :cols] + both[:, cols:] + dot(low, x[:, :cols], side, 0)

    def block(n, size=1):
        return pl.ds(n * B, size * B)

    def set_x(n, value):
        xs[block(n), :cols], xs[block(n), cols:] = split(value)

    def forward(a, d, size):
        span = pl.ds(d * B, size * B)
        return times(tile_hi[a, :, span], tile_lo[a, :, span], xs[block(a + d, size)], 1)

    def down(a):
        span = pl.ds(B, wide)
        return times(tile_hi[a, :, span], tile_lo[a, :, span], xs[block(a)], 0)

    def outgoing(sweep):
        acc[sweep, block(4, 3)] = down(3)
        low = down(2)
        acc[sweep, block(3)] = low[:B]
        acc[sweep, block(4, 2)] += low[B:]
        low = down(1)
        acc[sweep, block(2)] = low[:B]
        acc[sweep, block(3, 2)] += low[B:]
        return [
            move.to(acc.at[sweep, block(GROUP + n)], ret_in.at[sweep, n], after)
            for n in range(REACH_DEV)
        ]

    for slot in range(1, PLANES):
        from_plane(slot, (0, 1))
        cross[slot].own()
        cross[slot - 1].relay()
        if slot >= 2:
            cross[slot - 2].corner()
        if slot == 2:
            for copy in x_copies:
                copy.wait_recv()
            x_here.wait()
            halo_copy = move.to(xb.at[pl.ds(0, REACH_DEV)], halo, before)
    for slot in range(1, PLANES):
        from_plane(slot, (2,))
    edge.own()
    cross[0].ready()
    products(0)
    cross[3].relay()
    t_copies = share(target, tb)
    cross[2].corner()
    edge.relay()
    cross[1].ready()
    products(1)
    for n in range(GROUP):
        set_x(n, xb[n])
    cross[3].corner()
    edge.corner()
    halo_copy.wait_recv()
    for n in range(REACH_DEV):
        set_x(GROUP + n, halo[n])
    cross[2].ready()
    products(2)
    for copy in tab_copies:
        copy.wait_recv()
    cross[3].ready()
    products(3)

    rets = outgoing(0)
    acc[0, block(3)] += forward(3, 0, GROUP)
    acc[0, block(2)] += forward(2, 0, GROUP)
    acc[0, block(1)] = forward(1, 0, GROUP)
    edge.ready()
    edge_products()
    acc[0, block(1, 3)] += down(0)
    acc[0, block(0)] = forward(0, 0, GROUP)
    for copy in t_copies:
        copy.wait_recv()
    t_here.wait()

    aheads = []

    def advance(n):
        change = acc[0, block(n)]
        if n < REACH_DEV:
            rets[n].wait_recv()
            change = change + ret_in[0, n]
        px[n] = xb[n] + 0.5 * (tb[n] - xb[n] - change)
        if n < REACH_DEV:
            aheads.append(move.to(px.at[n], ahead.at[n], before))
        set_x(n, px[n])

    advance(3)
    for n in range(REACH_DEV):
        advance(n)
    rets = outgoing(1)
    acc[1, block(1)] = forward(1, 0, 3)
    acc[1, block(2)] += forward(2, 0, 2)
    acc[1, block(3)] += forward(3, 0, 1)
    acc[1, block(1, 3)] += down(0)
    acc[1, block(0)] = forward(0, 0, GROUP)

    base = move.reserve(GROUP)
    here_sem = local_sem.at[move.local]

    def leave(n, source):
        return move.make(final.at[n], out.at[:, piece(j)], chip(n), base + n, base + source)

    def stay(n):
        return pltpu.make_async_copy(final.at[n], out.at[:, piece(j)], here_sem)

    def put(n):
        change = acc[1, block(n)]
        if n < REACH_DEV:
            rets[n].wait_recv()
            change = change + ret_in[1, n]
        final[n] = px[n] + 0.5 * (tb[n] - px[n] - change)

        @pl.when(j != n)
        def _():
            leave(n, j).start()

        @pl.when(j == n)
        def _():
            stay(n).start()

    for n in range(REACH_DEV):
        aheads[n].wait_recv()
        set_x(GROUP + n, ahead[n])
        for a in range(n + 1, GROUP):
            acc[1, block(a)] += forward(a, GROUP + n - a, 1)
    for n in (3, 0, 1, 2):
        put(n)
    for n in range(GROUP):
        @pl.when(j != n)
        def _():
            leave(n, n).wait_send()
            leave(n, n).wait_recv()

        @pl.when(j == n)
        def _():
            stay(n).wait()
    for copy in move.open:
        copy.wait_send()


def in_one_kernel(perturb, pair_list, pair_count, band_weight, cov_scale, target, first_guess):
    w = gap_weights(pair_list, pair_count, band_weight, cov_scale)
    table = jnp.broadcast_to(jnp.pad(w, (0, 8 - w.shape[0]))[:, None], (8, BLOCK))
    rows = perturb.shape[0]
    cols = first_guess.shape[1] // GROUP
    members = 2 * GROUP * PLANES * rows
    f32, bf16 = jnp.float32, jnp.bfloat16
    sems = 112
    vmem = pl.BlockSpec(memory_space=pltpu.VMEM)
    anywhere = pl.BlockSpec(memory_space=pl.ANY)
    return pl.pallas_call(
        kernel,
        out_shape=jax.ShapeDtypeStruct(first_guess.shape, f32),
        in_specs=[anywhere, vmem, anywhere, anywhere],
        out_specs=vmem,
        scratch_shapes=[
            pltpu.VMEM((PLANES, GROUP, 2, rows, 2 * REACH_DEV * BLOCK), f32),
            pltpu.VMEM((GROUP, 2, PLANES, rows, BLOCK), f32),
            pltpu.VMEM((members, 2 * REACH_DEV * BLOCK), bf16),
            pltpu.VMEM((members, 2 * REACH_DEV * BLOCK), bf16),
            pltpu.VMEM((members, BLOCK), bf16),
            pltpu.VMEM((members, BLOCK), bf16),
            pltpu.VMEM((REACH_DEV, BLOCK, GROUP * BLOCK), f32),
            pltpu.VMEM((GROUP, BLOCK, GROUP * BLOCK), bf16),
            pltpu.VMEM((GROUP, BLOCK, GROUP * BLOCK), bf16),
            pltpu.VMEM((GROUP, 8, BLOCK), f32),
            pltpu.VMEM((GROUP, BLOCK, cols), f32),
            pltpu.VMEM((GROUP, BLOCK, cols), f32),
            pltpu.VMEM((REACH_DEV, BLOCK, cols), f32),
            pltpu.VMEM((NEAR * BLOCK, 2 * cols), bf16),
            pltpu.VMEM((2, NEAR * BLOCK, cols), f32),
            pltpu.VMEM((GROUP, BLOCK, cols), f32),
            pltpu.VMEM((2, REACH_DEV, BLOCK, cols), f32),
            pltpu.VMEM((REACH_DEV, BLOCK, cols), f32),
            pltpu.VMEM((GROUP, BLOCK, cols), f32),
            pltpu.SemaphoreType.DMA((sems,)),
            pltpu.SemaphoreType.DMA((sems,)),
            pltpu.SemaphoreType.DMA((8,)),
        ],
        compiler_params=pltpu.CompilerParams(
            collective_id=0, has_side_effects=True, vmem_limit_bytes=56 * 1024 * 1024
        ),
    )(perturb, table, first_guess, target)


def fits(perturb, field):
    return (
        lax.axis_size("mem") == 2 and lax.axis_size("space") == PLANES * GROUP
        and perturb.shape[0] % 16 == 0 and field.shape[1] % (GROUP * 128) == 0
        and field.shape[0] == BLOCK
    )


def per_device(perturb, pair_list, pair_count, band_weight, cov_scale, target, first_guess):
    whole = in_one_kernel if fits(perturb, first_guess) else by_collectives
    return whole(perturb, pair_list, pair_count, band_weight, cov_scale, target, first_guess)


def solution(mesh):
    in_specs = (
        P(("space", "mem"), None),
        P("space", None),
        P("space"),
        P(),
        P(),
        P("space", "mem"),
        P("space", "mem"),
    )
    out_specs = P("space", "mem")
    return jax.shard_map(
        per_device, mesh=mesh, in_specs=in_specs, out_specs=out_specs, check_vma=False
    )
```

time: 105 us -> 95.9 us (0.913)
  Pallas kernels: 97 us -> 89.6 us
  local copies, waits for them, and re-layouts: 4.67 us -> 3.22 us
    pallas_call x1, Pallas kernels: 97 us -> 89.6 us  [in_one_kernel(): pl.pallas_call(kernel, out_shape=jax.ShapeDtypeStruct(first_guess.shape,...]
    unnamed x11 -> x5, local copies, waits for them, and re-layouts: 4.59 us -> 2.54 us
where the time goes in v1:
time: 95.9 us; the launch traced here: 94.7 us
  Pallas kernels  89.6 us (93%)
  local copies, waits for them, and re-layouts  3.22 us (3%)
  between operations  1.34 us (1%)
    pallas_call x1, Pallas kernels, in_one_kernel(): pl.pallas_call(kernel, out_shape=jax.ShapeDtypeStruct(first_guess.shape,...  89.6 us
    unnamed x5, local copies, waits for them, and re-layouts  2.54 us

profile of v1, /device:TPU:8, one launch (start us, length us, event | category | flops | bytes accessed | tf_op | source)
XLA Modules:
  0.0 94.7 jit_solution(7402958557630964121)
XLA Ops:
  0.7 0.0 copy-start
  1.3 0.0 copy-done
  1.3 0.2 fusion.1
  1.6 0.0 copy-start.1
  1.6 0.7 copy-done.1
  2.2 0.2 select_reduce_fusion.1
  2.4 0.1 select_reduce_fusion
  2.5 0.7 broadcast_in_dim.39.table
  3.2 89.6 %shard_map.73 = f32[256,512]{1,0:T(8,128)} custom-call(f32[32,4096]{1,0:T(8,128)} %perturb.1, f32[8,256]{1,0:T(8,128)} %broadcast_in_dim.39.table, f32[256,512]{1,0:T(8,128)} %guess.1, f32[256,512]{1,0:T(8,128)} %target.1), custom_call_target="tpu_custom_call" | custom-call | tf_op jit(solution)/shard_map/pallas_call | solution.py:436
  92.8 1.9 %copy.11 = f32[256,512]{1,0:T(8,128)} copy(f32[256,512]{1,0:T(8,128)} %shard_map.73) | data formatting | bytes 1048576
  (2 shorter events, 0.0 us)
Async XLA Ops:
  0.7 0.7 copy-start
  1.6 0.7 copy-start.1

commit v2 on v1

--- a/solution.py
+++ b/solution.py
@@ -240,28 +240,34 @@
     def weight(a, d):
         return tabs[a, d : d + 1]
 
-    def products(r):
+    def pair(span, n, first, size):
+        own = pl.ds(pl.multiple_of(n * B, B), B)
+        row = pl.ds(pl.multiple_of((n + first) * B, B), size * B)
+        left = jnp.concatenate([chi[span, own], chi[span, own], clo[span, own]], 0)
+        right = jnp.concatenate([chi[span, row], clo[span, row], chi[span, row]], 0)
+        return dot(left, right, 0, 0)
+
+    def members(r):
         span = pl.ds(r * each, each)
         chi[span], clo[span] = split(gc[r].reshape(each, 2 * wide))
+        return span
+
+    def products(r):
+        span = members(r)
 
         def step(n, carry):
-            own = pl.ds(pl.multiple_of(n * B, B), B)
-            row = pl.ds(pl.multiple_of(n * B, B), inner)
-            left = jnp.concatenate([chi[span, own], chi[span, own], clo[span, own]], 0)
-            right = jnp.concatenate([chi[span, row], clo[span, row], chi[span, row]], 0)
-            value = dot(left, right, 0, 0)
-            if r > 0:
-                value = value + part[n]
-            if r < PLANES - 1:
-                part[n] = value
-            else:
-                for d in range(GROUP):
-                    now = value[:, d * B : (d + 1) * B] * weight(n + 1, d)
-                    there = pl.ds(d * B, B)
-                    tile_hi[n + 1, :, there], tile_lo[n + 1, :, there] = split(now)
+            value = pair(span, n, 0, GROUP)
+            part[n] = value if r == 0 else part[n] + value
             return carry
 
         lax.fori_loop(0, REACH_DEV, step, 0)
+
+    def finish(span, a, first, size):
+        value = pair(span, a - 1, first, size) + part[a - 1, :, pl.ds(first * B, size * B)]
+        for d in range(size):
+            now = value[:, d * B : (d + 1) * B] * weight(a, first + d)
+            there = pl.ds((first + d) * B, B)
+            tile_hi[a, :, there], tile_lo[a, :, there] = split(now)
 
     def edge_products():
         for r in range(PLANES):
@@ -292,22 +298,25 @@
         span = pl.ds(d * B, size * B)
         return times(tile_hi[a, :, span], tile_lo[a, :, span], xs[block(a + d, size)], 1)
 
-    def down(a):
-        span = pl.ds(B, wide)
+    def down(a, first, size):
+        span = pl.ds(first * B, size * B)
         return times(tile_hi[a, :, span], tile_lo[a, :, span], xs[block(a)], 0)
 
-    def outgoing(sweep):
-        acc[sweep, block(4, 3)] = down(3)
-        low = down(2)
-        acc[sweep, block(3)] = low[:B]
-        acc[sweep, block(4, 2)] += low[B:]
-        low = down(1)
-        acc[sweep, block(2)] = low[:B]
-        acc[sweep, block(3, 2)] += low[B:]
-        return [
-            move.to(acc.at[sweep, block(GROUP + n)], ret_in.at[sweep, n], after)
-            for n in range(REACH_DEV)
-        ]
+    def outgoing(sweep, ready):
+        copies = {}
+        for n in range(REACH_DEV - 1, -1, -1):
+            a = n + 1
+            ready(a)
+            value = down(a, GROUP - a, a)
+            if a == REACH_DEV:
+                acc[sweep, block(GROUP, a)] = value
+            else:
+                acc[sweep, block(GROUP, a)] += value
+            copies[n] = move.to(acc.at[sweep, block(GROUP + n)], ret_in.at[sweep, n], after)
+        return copies
+
+    def inside(sweep, a):
+        acc[sweep, block(a + 1, REACH_DEV - a)] += down(a, 1, REACH_DEV - a)
 
     for slot in range(1, PLANES):
         from_plane(slot, (0, 1))
@@ -323,61 +332,65 @@
     for slot in range(1, PLANES):
         from_plane(slot, (2,))
     edge.own()
+    for n in range(GROUP):
+        set_x(n, xb[n])
     cross[0].ready()
     products(0)
-    cross[3].relay()
-    t_copies = share(target, tb)
-    cross[2].corner()
-    edge.relay()
     cross[1].ready()
     products(1)
-    for n in range(GROUP):
-        set_x(n, xb[n])
-    cross[3].corner()
-    edge.corner()
+    cross[3].relay()
+    cross[2].corner()
+    cross[2].ready()
+    products(2)
+    edge.relay()
+    t_copies = share(target, tb)
     halo_copy.wait_recv()
     for n in range(REACH_DEV):
         set_x(GROUP + n, halo[n])
-    cross[2].ready()
-    products(2)
     for copy in tab_copies:
         copy.wait_recv()
+    cross[3].corner()
     cross[3].ready()
-    products(3)
-
-    rets = outgoing(0)
-    acc[0, block(3)] += forward(3, 0, GROUP)
-    acc[0, block(2)] += forward(2, 0, GROUP)
-    acc[0, block(1)] = forward(1, 0, GROUP)
+    last = members(PLANES - 1)
+    for a in range(REACH_DEV, 0, -1):
+        finish(last, a, GROUP - a, a)
+    rets = outgoing(0, lambda a: None)
+    for a in range(1, GROUP):
+        finish(last, a, 0, GROUP - a)
+    for a in range(1, GROUP):
+        acc[0, block(a)] = forward(a, 0, GROUP)
+    inside(0, 1)
+    inside(0, 2)
+    edge.corner()
     edge.ready()
     edge_products()
-    acc[0, block(1, 3)] += down(0)
+    inside(0, 0)
     acc[0, block(0)] = forward(0, 0, GROUP)
     for copy in t_copies:
         copy.wait_recv()
     t_here.wait()
 
     aheads = []
-
-    def advance(n):
-        change = acc[0, block(n)]
+    for n in range(GROUP):
+        px[n] = xb[n] + 0.5 * (tb[n] - xb[n] - acc[0, block(n)])
+        if n < REACH_DEV:
+            aheads.append(move.to(px.at[n], ahead.at[n], before))
+    set_x(REACH_DEV, px[REACH_DEV])
+    final[REACH_DEV] = px[REACH_DEV]
+
+    def settle(n):
         if n < REACH_DEV:
             rets[n].wait_recv()
-            change = change + ret_in[0, n]
-        px[n] = xb[n] + 0.5 * (tb[n] - xb[n] - change)
-        if n < REACH_DEV:
-            aheads.append(move.to(px.at[n], ahead.at[n], before))
-        set_x(n, px[n])
-
-    advance(3)
-    for n in range(REACH_DEV):
-        advance(n)
-    rets = outgoing(1)
-    acc[1, block(1)] = forward(1, 0, 3)
-    acc[1, block(2)] += forward(2, 0, 2)
-    acc[1, block(3)] += forward(3, 0, 1)
-    acc[1, block(1, 3)] += down(0)
-    acc[1, block(0)] = forward(0, 0, GROUP)
+            now = px[n] - 0.5 * ret_in[0, n]
+            set_x(n, now)
+            final[n] = now
+
+    rets_last = outgoing(1, settle)
+    settle(0)
+    for a in range(GROUP):
+        acc[1, block(a)] = forward(a, 0, GROUP - a)
+    for a in range(REACH_DEV):
+        inside(1, a)
 
     base = move.reserve(GROUP)
     here_sem = local_sem.at[move.local]
@@ -391,9 +404,9 @@
     def put(n):
         change = acc[1, block(n)]
         if n < REACH_DEV:
-            rets[n].wait_recv()
+            rets_last[n].wait_recv()
             change = change + ret_in[1, n]
-        final[n] = px[n] + 0.5 * (tb[n] - px[n] - change)
+        final[n] = final[n] + 0.5 * (tb[n] - final[n] - change)
 
         @pl.when(j != n)
         def _():
@@ -405,10 +418,10 @@
 
     for n in range(REACH_DEV):
         aheads[n].wait_recv()
-        set_x(GROUP + n, ahead[n])
+        set_x(GROUP + n, ahead[n] - 0.5 * acc[0, block(GROUP + n)])
         for a in range(n + 1, GROUP):
             acc[1, block(a)] += forward(a, GROUP + n - a, 1)
-    for n in (3, 0, 1, 2):
+    for n in (3, 2, 1, 0):
         put(n)
     for n in range(GROUP):
         @pl.when(j != n)

time: 95.9 us -> 90.6 us (0.945)
  Pallas kernels: 89.6 us -> 84.2 us
    pallas_call x1, Pallas kernels: 89.6 us -> 84.2 us  [in_one_kernel(): pl.pallas_call(kernel, out_shape=jax.ShapeDtypeStruct(first_guess.shape,...]
where the time goes in v2:
time: 90.6 us; the launch traced here: 89.2 us
  Pallas kernels  84.2 us (93%)
  local copies, waits for them, and re-layouts  3.22 us (4%)
  between operations  1.34 us (1%)
    pallas_call x1, Pallas kernels, in_one_kernel(): pl.pallas_call(kernel, out_shape=jax.ShapeDtypeStruct(first_guess.shape,...  84.2 us
    unnamed x5, local copies, waits for them, and re-layouts  2.54 us

profile of v2, /device:TPU:8, one launch (start us, length us, event | category | flops | bytes accessed | tf_op | source)
XLA Modules:
  0.0 89.2 jit_solution(12866900115303550931)
XLA Ops:
  0.7 0.0 copy-start
  1.3 0.0 copy-done
  1.3 0.2 fusion.1
  1.6 0.0 copy-start.1
  1.6 0.7 copy-done.1
  2.2 0.2 select_reduce_fusion.1
  2.4 0.1 select_reduce_fusion
  2.5 0.7 broadcast_in_dim.39.table
  3.2 84.2 %shard_map.73 = f32[256,512]{1,0:T(8,128)} custom-call(f32[32,4096]{1,0:T(8,128)} %perturb.1, f32[8,256]{1,0:T(8,128)} %broadcast_in_dim.39.table, f32[256,512]{1,0:T(8,128)} %guess.1, f32[256,512]{1,0:T(8,128)} %target.1), custom_call_target="tpu_custom_call" | custom-call | tf_op jit(solution)/shard_map/pallas_call | solution.py:449
  87.3 1.9 %copy.11 = f32[256,512]{1,0:T(8,128)} copy(f32[256,512]{1,0:T(8,128)} %shard_map.73) | data formatting | bytes 1048576
  (2 shorter events, 0.0 us)
Async XLA Ops:
  0.7 0.7 copy-start
  1.6 0.7 copy-start.1

commit v3 on v2

--- a/solution.py
+++ b/solution.py
@@ -115,7 +115,7 @@
 
 
 def kernel(perturb, table, guess, target, out, gc, gb, chi, clo, bhi, blo, part, tile_hi, tile_lo,
-           tabs, xb, tb, halo, xs, acc, px, ret_in, ahead, final, send_sem, recv_sem, local_sem):
+           tabs, xb, tb, halo, xs, acc, px, ret_in, ahead, final, via, send_sem, recv_sem, local_sem):
     space = lax.axis_index("space")
     mem = lax.axis_index("mem")
     k = space // GROUP
@@ -227,14 +227,30 @@
     tab_here.wait()
     tab_copies = [move.to(tabs.at[j], tabs.at[j], chip((j + q) % GROUP)) for q in range(1, GROUP)]
 
-    def share(source, blocks):
-        copies = []
-        for q in range(1, GROUP):
-            there = (j + q) % GROUP
-            copies.append(move.to(source.at[:, piece(there)], blocks.at[j], chip(there)))
-        return copies
-
-    x_copies = share(guess, xb)
+    jx = j + 1 - 2 * (j % 2)
+    jy = (j + 2) % GROUP
+    jd = (jx + 2) % GROUP
+    top, bottom = pl.ds(0, B // 2), pl.ds(B // 2, B // 2)
+
+    class Share:
+        def __init__(self, source, blocks, via):
+            self.blocks, self.via = blocks, via
+            self.first = move.to(source.at[top, piece(jd)], via.at[0], xn)
+            self.second = move.to(source.at[bottom, piece(jd)], via.at[1], yn)
+            self.done = [move.to(source.at[:, piece(jx)], blocks.at[j], xn),
+                         move.to(source.at[:, piece(jy)], blocks.at[j], yn)]
+
+        def relay(self):
+            self.first.wait_recv()
+            self.done.append(move.to(self.via.at[0], self.blocks.at[jx, top], yn))
+            self.second.wait_recv()
+            self.done.append(move.to(self.via.at[1], self.blocks.at[jy, bottom], xn))
+
+        def ready(self):
+            for copy in self.done:
+                copy.wait_recv()
+
+    x_share = Share(guess, xb, via.at[0])
     exchange((2,))
 
     def weight(a, d):
@@ -322,11 +338,12 @@
         from_plane(slot, (0, 1))
         cross[slot].own()
         cross[slot - 1].relay()
+        if slot == 1:
+            x_share.relay()
         if slot >= 2:
             cross[slot - 2].corner()
         if slot == 2:
-            for copy in x_copies:
-                copy.wait_recv()
+            x_share.ready()
             x_here.wait()
             halo_copy = move.to(xb.at[pl.ds(0, REACH_DEV)], halo, before)
     for slot in range(1, PLANES):
@@ -343,7 +360,7 @@
     cross[2].ready()
     products(2)
     edge.relay()
-    t_copies = share(target, tb)
+    t_share = Share(target, tb, via.at[1])
     halo_copy.wait_recv()
     for n in range(REACH_DEV):
         set_x(GROUP + n, halo[n])
@@ -355,6 +372,7 @@
     for a in range(REACH_DEV, 0, -1):
         finish(last, a, GROUP - a, a)
     rets = outgoing(0, lambda a: None)
+    t_share.relay()
     for a in range(1, GROUP):
         finish(last, a, 0, GROUP - a)
     for a in range(1, GROUP):
@@ -366,8 +384,7 @@
     edge_products()
     inside(0, 0)
     acc[0, block(0)] = forward(0, 0, GROUP)
-    for copy in t_copies:
-        copy.wait_recv()
+    t_share.ready()
     t_here.wait()
 
     aheads = []
@@ -471,6 +488,7 @@
             pltpu.VMEM((2, REACH_DEV, BLOCK, cols), f32),
             pltpu.VMEM((REACH_DEV, BLOCK, cols), f32),
             pltpu.VMEM((GROUP, BLOCK, cols), f32),
+            pltpu.VMEM((2, 2, BLOCK // 2, cols), f32),
             pltpu.SemaphoreType.DMA((sems,)),
             pltpu.SemaphoreType.DMA((sems,)),
             pltpu.SemaphoreType.DMA((8,)),

time: 90.6 us -> 90.9 us (level); the launches traced: 89.2 us -> 90.6 us
  Pallas kernels: 84.2 us -> 85.6 us
    pallas_call x1, Pallas kernels: 84.2 us -> 85.6 us  [in_one_kernel(): pl.pallas_call(kernel, out_shape=jax.ShapeDtypeStruct(first_guess.shape,...]
where the time goes in v3:
time: 90.9 us; the launch traced here: 90.6 us
  Pallas kernels  85.6 us (94%)
  local copies, waits for them, and re-layouts  3.22 us (4%)
  between operations  1.34 us (1%)
    pallas_call x1, Pallas kernels, in_one_kernel(): pl.pallas_call(kernel, out_shape=jax.ShapeDtypeStruct(first_guess.shape,...  85.6 us
    unnamed x5, local copies, waits for them, and re-layouts  2.54 us

profile of v3, /device:TPU:8, one launch (start us, length us, event | category | flops | bytes accessed | tf_op | source)
XLA Modules:
  0.0 90.6 jit_solution(17899515833059591643)
XLA Ops:
  0.7 0.0 copy-start
  1.3 0.0 copy-done
  1.3 0.2 fusion.1
  1.6 0.0 copy-start.1
  1.6 0.7 copy-done.1
  2.2 0.2 select_reduce_fusion.1
  2.4 0.1 select_reduce_fusion
  2.5 0.7 broadcast_in_dim.39.table
  3.2 85.6 %shard_map.73 = f32[256,512]{1,0:T(8,128)} custom-call(f32[32,4096]{1,0:T(8,128)} %perturb.1, f32[8,256]{1,0:T(8,128)} %broadcast_in_dim.39.table, f32[256,512]{1,0:T(8,128)} %guess.1, f32[256,512]{1,0:T(8,128)} %target.1), custom_call_target="tpu_custom_call" | custom-call | tf_op jit(solution)/shard_map/pallas_call | solution.py:466
  88.8 1.9 %copy.11 = f32[256,512]{1,0:T(8,128)} copy(f32[256,512]{1,0:T(8,128)} %shard_map.73) | data formatting | bytes 1048576
  (2 shorter events, 0.0 us)
Async XLA Ops:
  0.7 0.7 copy-start
  1.6 0.7 copy-start.1

commit v4 on v3

--- a/solution.py
+++ b/solution.py
@@ -340,9 +340,12 @@
         cross[slot - 1].relay()
         if slot == 1:
             x_share.relay()
+            t_share = Share(target, tb, via.at[1])
         if slot >= 2:
             cross[slot - 2].corner()
         if slot == 2:
+            t_share.relay()
+        if slot == 3:
             x_share.ready()
             x_here.wait()
             halo_copy = move.to(xb.at[pl.ds(0, REACH_DEV)], halo, before)
@@ -360,7 +363,6 @@
     cross[2].ready()
     products(2)
     edge.relay()
-    t_share = Share(target, tb, via.at[1])
     halo_copy.wait_recv()
     for n in range(REACH_DEV):
         set_x(GROUP + n, halo[n])
@@ -372,7 +374,6 @@
     for a in range(REACH_DEV, 0, -1):
         finish(last, a, GROUP - a, a)
     rets = outgoing(0, lambda a: None)
-    t_share.relay()
     for a in range(1, GROUP):
         finish(last, a, 0, GROUP - a)
     for a in range(1, GROUP):

time: 90.9 us -> 96.5 us (1.062)
  Pallas kernels: 85.6 us -> 91.2 us
    pallas_call x1, Pallas kernels: 85.6 us -> 91.2 us  [in_one_kernel(): pl.pallas_call(kernel, out_shape=jax.ShapeDtypeStruct(first_guess.shape,...]
where the time goes in v4:
time: 96.5 us; the launch traced here: 96.2 us
  Pallas kernels  91.2 us (95%)
  local copies, waits for them, and re-layouts  3.22 us (3%)
  between operations  1.34 us (1%)
    pallas_call x1, Pallas kernels, in_one_kernel(): pl.pallas_call(kernel, out_shape=jax.ShapeDtypeStruct(first_guess.shape,...  91.2 us
    unnamed x5, local copies, waits for them, and re-layouts  2.54 us

profile of v4, /device:TPU:8, one launch (start us, length us, event | category | flops | bytes accessed | tf_op | source)
XLA Modules:
  0.0 96.2 jit_solution(4944010715164525271)
XLA Ops:
  0.7 0.0 copy-start
  1.3 0.0 copy-done
  1.3 0.2 fusion.1
  1.6 0.0 copy-start.1
  1.6 0.7 copy-done.1
  2.2 0.2 select_reduce_fusion.1
  2.4 0.1 select_reduce_fusion
  2.5 0.7 broadcast_in_dim.39.table
  3.2 91.2 %shard_map.73 = f32[256,512]{1,0:T(8,128)} custom-call(f32[32,4096]{1,0:T(8,128)} %perturb.1, f32[8,256]{1,0:T(8,128)} %broadcast_in_dim.39.table, f32[256,512]{1,0:T(8,128)} %guess.1, f32[256,512]{1,0:T(8,128)} %target.1), custom_call_target="tpu_custom_call" | custom-call | tf_op jit(solution)/shard_map/pallas_call | solution.py:467
  94.4 1.9 %copy.11 = f32[256,512]{1,0:T(8,128)} copy(f32[256,512]{1,0:T(8,128)} %shard_map.73) | data formatting | bytes 1048576
  (2 shorter events, 0.0 us)
Async XLA Ops:
  0.7 0.7 copy-start
  1.6 0.7 copy-start.1

commit v5 on v3

--- a/solution.py
+++ b/solution.py
@@ -114,8 +114,9 @@
         return copy
 
 
-def kernel(perturb, table, guess, target, out, gc, gb, chi, clo, bhi, blo, part, tile_hi, tile_lo,
-           tabs, xb, tb, halo, xs, acc, px, ret_in, ahead, final, via, send_sem, recv_sem, local_sem):
+def kernel(perturb, pair_list, pair_count, band_weight, cov_scale, guess, target, out, gc, gb, chi, clo, bhi, blo, part, tile_hi, tile_lo,
+           tabs, xb, tb, halo, xs, acc, px, ret_in, ahead, final, via, pairs, live, bands,
+           scale, send_sem, recv_sem, local_sem):
     space = lax.axis_index("space")
     mem = lax.axis_index("mem")
     k = space // GROUP
@@ -166,7 +167,8 @@
     own_here = [move.here(*pair) for pair in pieces(k, 0)]
     x_here = move.here(guess.at[:, piece(j)], xb.at[j])
     t_here = move.here(target.at[:, piece(j)], tb.at[j])
-    tab_here = move.here(table, tabs.at[j])
+    small = [move.here(pair_list, pairs), move.here(pair_count, live),
+             move.here(band_weight, bands), move.here(cov_scale, scale)]
     pl.semaphore_wait(barrier, len(greeted))
 
     zsem = move.reserve(3 * PLANES)
@@ -224,7 +226,22 @@
     cross = [Gather(gc.at[r], half) for r in range(PLANES)]
     edge = Gather(gb, PLANES // 2)
     cross[0].own()
-    tab_here.wait()
+    for copy in small:
+        copy.wait()
+    sums = [0.0] * GROUP
+    for n in range(pairs.shape[0]):
+        gap = (pairs[n, 1] - pairs[n, 0] + PLANES * GROUP) % (PLANES * GROUP)
+        band = pairs[n, 2]
+        rate = jnp.float32(0.0)
+        for c in range(NBANDS):
+            rate = jnp.where(band == c, bands[c], rate)
+        rate = jnp.where(n < live[0], rate * scale[0], 0.0)
+        sums = [jnp.where(gap == d, rate, sums[d]) for d in range(GROUP)]
+    line = lax.broadcasted_iota(jnp.int32, (8, B), 0)
+    rates = jnp.zeros((8, B), jnp.float32)
+    for d in range(GROUP):
+        rates = jnp.where(line == d, sums[d], rates)
+    tabs[j] = rates / (MEMBERS - 1)
     tab_copies = [move.to(tabs.at[j], tabs.at[j], chip((j + q) % GROUP)) for q in range(1, GROUP)]
 
     jx = j + 1 - 2 * (j % 2)
@@ -361,9 +378,6 @@
     products(2)
     edge.relay()
     t_share = Share(target, tb, via.at[1])
-    halo_copy.wait_recv()
-    for n in range(REACH_DEV):
-        set_x(GROUP + n, halo[n])
     for copy in tab_copies:
         copy.wait_recv()
     cross[3].corner()
@@ -373,6 +387,9 @@
         finish(last, a, GROUP - a, a)
     rets = outgoing(0, lambda a: None)
     t_share.relay()
+    halo_copy.wait_recv()
+    for n in range(REACH_DEV):
+        set_x(GROUP + n, halo[n])
     for a in range(1, GROUP):
         finish(last, a, 0, GROUP - a)
     for a in range(1, GROUP):
@@ -454,8 +471,6 @@
 
 
 def in_one_kernel(perturb, pair_list, pair_count, band_weight, cov_scale, target, first_guess):
-    w = gap_weights(pair_list, pair_count, band_weight, cov_scale)
-    table = jnp.broadcast_to(jnp.pad(w, (0, 8 - w.shape[0]))[:, None], (8, BLOCK))
     rows = perturb.shape[0]
     cols = first_guess.shape[1] // GROUP
     members = 2 * GROUP * PLANES * rows
@@ -466,7 +481,7 @@
     return pl.pallas_call(
         kernel,
         out_shape=jax.ShapeDtypeStruct(first_guess.shape, f32),
-        in_specs=[anywhere, vmem, anywhere, anywhere],
+        in_specs=[anywhere] * 7,
         out_specs=vmem,
         scratch_shapes=[
             pltpu.VMEM((PLANES, GROUP, 2, rows, 2 * REACH_DEV * BLOCK), f32),
@@ -489,14 +504,18 @@
             pltpu.VMEM((REACH_DEV, BLOCK, cols), f32),
             pltpu.VMEM((GROUP, BLOCK, cols), f32),
             pltpu.VMEM((2, 2, BLOCK // 2, cols), f32),
+            pltpu.SMEM(pair_list.shape, jnp.int32),
+            pltpu.SMEM(pair_count.shape, jnp.int32),
+            pltpu.SMEM(band_weight.shape, f32),
+            pltpu.SMEM(cov_scale.shape, f32),
             pltpu.SemaphoreType.DMA((sems,)),
             pltpu.SemaphoreType.DMA((sems,)),
-            pltpu.SemaphoreType.DMA((8,)),
+            pltpu.SemaphoreType.DMA((16,)),
         ],
         compiler_params=pltpu.CompilerParams(
             collective_id=0, has_side_effects=True, vmem_limit_bytes=56 * 1024 * 1024
         ),
-    )(perturb, table, first_guess, target)
+    )(perturb, pair_list, pair_count, band_weight, cov_scale, first_guess, target)
 
 
 def fits(perturb, field):

time: 90.9 us -> 88.4 us (0.972)
  local copies, waits for them, and re-layouts: 3.22 us -> 1.87 us
    unnamed x5 -> x1, local copies, waits for them, and re-layouts: 2.54 us -> 1.87 us
where the time goes in v5:
time: 88.4 us; the launch traced here: 88.2 us
  Pallas kernels  85 us (96%)
  local copies, waits for them, and re-layouts  1.87 us (2%)
  between operations  1.3 us (1%)
    pallas_call x1, Pallas kernels, in_one_kernel(): pl.pallas_call(kernel, out_shape=jax.ShapeDtypeStruct(first_guess.shape,...  85 us
    unnamed x1, local copies, waits for them, and re-layouts  1.87 us

profile of v5, /device:TPU:8, one launch (start us, length us, event | category | flops | bytes accessed | tf_op | source)
XLA Modules:
  0.0 88.2 jit_solution(5193876659255739537)
XLA Ops:
  1.3 85.0 %shard_map.73 = f32[256,512]{1,0:T(8,128)} custom-call(f32[32,4096]{1,0:T(8,128)} %perturb.1, s32[4,3]{1,0:T(4,128)} %pair_list.1, s32[1]{0:T(128)S(6)} %copy.9.pair_count, f32[8]{0:T(128)} %band_weight.1, f32[1]{0:T(128)S(6)} %copy.10.cov_scale, f32[256,512]{1,0:T(8,128)} %guess.1, f32[256,512]{1,0:T(8,128)} %target.1), custom_call_target="tpu_custom_call" | custom-call | tf_op jit(solution)/shard_map/pallas_call | solution.py:481
  86.3 1.9 %copy.11 = f32[256,512]{1,0:T(8,128)} copy(f32[256,512]{1,0:T(8,128)} %shard_map.73) | data formatting | bytes 1048576
